TPU v7x, 32 devices: a whole 2x2x4 slice. The times are simulated.
32 devices in a mesh: groups: 2 (over y), wide: 16 (over z, x, core).
Axes of the slice: x: 2, y: 2, z: 4, core: 2. Of those that a mesh axis runs over, the one named last changes fastest.
Arguments:
- fields: bfloat16 [32, 512], P(('groups', 'wide')), parts along dimension 0, may hold values from -6 to 6
- chol: bfloat16 [512, 1024, 1024], P(None, 'wide'), may hold values from -0.01171875 to 0.01171875
- orbitals: bfloat16 [32, 1024, 256], P(('groups', 'wide')), parts along dimension 0, may hold values from -6 to 6
- trial: bfloat16 [1024, 256], replicated, may hold values from -0.5 to 0.5
Outputs:
- new_orbitals: bfloat16 [32, 1024, 256], P(('groups', 'wide')), parts along dimension 0
- force_bias: float32 [32, 2, 512], P(('groups', 'wide')), parts along dimension 0
There are 2 independent parts, one for each index of `groups`. A program takes and returns all parts, laid end to end along the dimension named above; an argument that names none is the same for every part. Nothing has to cross between parts.
All inputs are finite; a program needn't handle non-finite values.
Results may differ from a plain program's by a relative error of at most 0.0075.
Values may be sent and summed in bfloat16 or wider, within the bound.
No kernel may reach another device: no remote copies, remote signals or barrier semaphores. Data moves between devices by JAX's collectives and lax.ppermute only.
A program may use at most 192 MiB of HBM per device.

v0:
```python
import jax
import jax.numpy as jnp
from jax import lax
from jax.sharding import PartitionSpec as P

TAYLOR = 4


def per_device(fields, chol, orbitals, trial):
    all_fields = lax.all_gather(fields, "wide", axis=0, tiled=True)
    vectors, rows, width = chol.shape
    chol_flat = chol.reshape(vectors, rows * width)
    generator = jnp.dot(all_fields, chol_flat, preferred_element_type=jnp.float32).astype(
        jnp.bfloat16
    )
    generator = generator.reshape(all_fields.shape[0], rows, width)
    owned = lax.all_to_all(generator, "wide", split_axis=0, concat_axis=1, tiled=True)
    nocc = orbitals.shape[2] // 2
    walk_local = orbitals.shape[0]
    gen_walker = owned[0]
    total = orbitals[0].astype(jnp.float32)
    operand = orbitals[0]
    for order in range(1, TAYLOR + 1):
        product = jnp.dot(gen_walker, operand, preferred_element_type=jnp.float32)
        term = jnp.concatenate([-product[:, nocc:], product[:, :nocc]], axis=1) / order
        total = total + term
        if order < TAYLOR:
            operand = term.astype(jnp.bfloat16)
    fresh_list = [total.astype(jnp.bfloat16)]
    new_orbitals = jnp.stack(fresh_list, axis=0)
    trial_real = trial[:, :nocc].T
    trial_imag = trial[:, nocc:].T
    mixer = jnp.concatenate(
        [
            jnp.concatenate([trial_real, -trial_imag], axis=1),
            jnp.concatenate([trial_imag, trial_real], axis=1),
        ],
        axis=0,
    )
    orbital_rows = lax.all_to_all(new_orbitals, "wide", split_axis=1, concat_axis=0, tiled=True)
    count = orbital_rows.shape[0]
    flat_rows = orbital_rows.reshape(count * rows, 2 * nocc)
    tile_green = jnp.dot(flat_rows, mixer, preferred_element_type=jnp.float32).astype(jnp.bfloat16)
    tile_green = tile_green.reshape(count, rows, 2 * width)
    all_walk = tile_green.shape[0]
    tile_green = (
        tile_green.reshape(all_walk, rows, 2, width)
        .transpose(0, 2, 1, 3)
        .reshape(all_walk * 2, rows * width)
    )
    partial_value = jnp.dot(tile_green, chol_flat.T, preferred_element_type=jnp.float32).reshape(
        all_walk, 2, vectors
    )
    summed = lax.psum(partial_value, "wide")
    force_bias = lax.dynamic_slice_in_dim(
        summed, lax.axis_index("wide") * walk_local, walk_local, 0
    )
    return (new_orbitals, force_bias)


def solution(mesh):
    in_specs = (
        P(("groups", "wide"), None),
        P(None, "wide", None),
        P(("groups", "wide"), None, None),
        P(),
    )
    out_specs = (P(("groups", "wide"), None, None), P(("groups", "wide"), None, None))
    return jax.shard_map(
        per_device, mesh=mesh, in_specs=in_specs, out_specs=out_specs, check_vma=False
    )
```

profile of v0, /device:TPU:8, one launch (start us, length us, event | category | flops | bytes accessed | tf_op | source)
XLA Modules:
  0.0 381.3 jit_solution(17390543338026890626)
XLA Ops:
  7.2 58.5 %copy.31 = bf16[64,8,64,1024]{3,1,2,0:T(8,128)(2,1)} copy(bf16[64,8,64,1024]{3,2,1,0:T(8,128)(2,1)} %bitcast.19) | data formatting | bytes 134217728
  65.7 18.9 %all-gather = bf16[16,1,512]{2,1,0:T(2,128)(2,1)S(1)} all-gather(bf16[1,1,512]{2,1,0:T(2,128)(2,1)S(1)} %bitcast.65), channel_id=1, replica_groups=mesh['groups'=2,'wide'=16] {'wide'}, dimensions={0}, use_global_device_ids=true | all-gather | bytes 17408 | tf_op jit(solution)/shard_map/all_gather | solution.py:10
  84.6 22.8 %convolution_convert_fusion = bf16[16,65536]{1,0:T(8,128)(2,1)S(1)} fusion(bf16[512,65536]{1,0:T(8,128)(2,1)} %bitcast.20, bf16[16,1,512]{2,1,0:T(2,128)(2,1)S(1)} %all-gather), kind=kOutput, calls=%fused_computation | convolution fusion | flops 1074790400 | bytes 69222400 | tf_op jit(solution)/shard_map/dot_general | solution.py:13
  107.4 2.5 copy.32
  109.9 6.9 %all-to-all-start = ((bf16[16,64,1024]{2,1,0:T(8,128)(2,1)}), bf16[16,64,1024]{2,1,0:T(8,128)(2,1)S(1)}, u32[]{:S(2)}, u32[]{:S(2)}) async-start(bf16[16,64,1024]{2,1,0:T(8,128)(2,1)} %bitcast.62), calls=%async_computation | async-start | bytes 4194304 | tf_op jit(solution)/shard_map/all_to_all | solution.py:17
  116.8 0.2 copy.22
  117.0 45.6 %all-to-all-done = bf16[16,64,1024]{2,1,0:T(8,128)(2,1)S(1)} async-done(((bf16[16,64,1024]{2,1,0:T(8,128)(2,1)}), bf16[16,64,1024]{2,1,0:T(8,128)(2,1)S(1)}, u32[]{:S(2)}, u32[]{:S(2)}) %all-to-all-start) | async-done | bytes 2097184 | tf_op jit(solution)/shard_map/all_to_all | solution.py:17
  162.7 0.8 fusion.34
  163.4 0.1 fusion.38
  163.6 0.7 fusion.28
  164.3 0.1 slice_negate_fusion.2
  164.5 0.7 fusion.25
  165.2 0.1 slice_negate_fusion.1
  165.4 0.7 fusion.23
  166.1 0.1 fusion.27
  166.2 0.6 fusion.13
  166.8 0.9 copy.23
  167.7 0.5 broadcast.24
  168.2 3.8 %reduce = bf16[1024,256]{1,0:T(8,128)(2,1)S(1)} reduce(bf16[1024,1,256]{2,1,0:T(2,128)(2,1)S(1)} %bitcast.63, bf16[]{:T(256)} %broadcast.24), dimensions={1}, to_apply=%bitcast.50.reduce_sub_computation | reduce | bytes 1048578
  172.0 0.9 reshape.121
  172.9 6.4 %all-to-all-start.1 = ((bf16[16,2,8192]{2,1,0:T(2,128)(2,1)}), bf16[16,2,8192]{2,1,0:T(2,128)(2,1)S(1)}, u32[]{:S(2)}, u32[]{:S(2)}) async-start(bf16[16,2,8192]{2,1,0:T(2,128)(2,1)} %reshape.121), calls=%async_computation.1 | async-start | bytes 1048576 | tf_op jit(solution)/shard_map/all_to_all | solution.py:40
  179.3 0.0 all-reduce.2.cloned.1.call-start
  179.4 13.3 %all-to-all-done.1 = bf16[16,2,8192]{2,1,0:T(2,128)(2,1)S(1)} async-done(((bf16[16,2,8192]{2,1,0:T(2,128)(2,1)}), bf16[16,2,8192]{2,1,0:T(2,128)(2,1)S(1)}, u32[]{:S(2)}, u32[]{:S(2)}) %all-to-all-start.1) | async-done | bytes 524320 | tf_op jit(solution)/shard_map/all_to_all | solution.py:40
  192.8 0.5 reshape.122
  193.3 3.3 convolution_convert_fusion.1
  196.6 7.8 %reshape_reshape.3 = bf16[16,64,2,1024]{3,2,1,0:T(2,128)(2,1)} reshape(bf16[1024,2048]{1,0:T(8,128)(2,1)} %convolution_convert_fusion.1) | data formatting | bytes 8388608 | tf_op jit(solution)/shard_map/reshape;reshape | solution.py:47
  204.3 80.0 %fusion.5 = f32[16,2,512]{2,0,1:T(8,128)} fusion(bf16[512,64,1024]{2,1,0:T(8,128)(2,1)} %param.5, bf16[16,64,2,1024]{3,2,1,0:T(2,128)(2,1)} %reshape_reshape.3), kind=kOutput, calls=%fused_computation.7 | convolution fusion | flops 2147483648 | bytes 71368704 | tf_op jit(solution)/shard_map/dot_general | solution.py:51
  284.3 0.0 all-reduce.2.cloned.1.call-update
  284.3 1.0 copy.26
  285.3 87.8 %all-reduce.2.cloned.1.call-done = f32[16,2,512]{2,0,1:T(8,128)} async-done(((f32[16,2,512]{2,0,1:T(8,128)}), f32[16,2,512]{2,0,1:T(8,128)}) %all-reduce.2.cloned.1.call-update) | async-done | bytes 65552 | tf_op jit(solution)/shard_map/psum | solution.py:54
  373.1 0.8 constant_dynamic-slice_fusion
  373.9 0.6 copy.27
  (9 shorter events, 0.1 us)
Async XLA Ops:
  7.2 58.6 %copy-start.2 = (bf16[1,512]{1,0:T(2,128)(2,1)S(1)}, bf16[1,512]{1,0:T(2,128)(2,1)}, u32[]{:S(2)}) copy-start(bf16[1,512]{1,0:T(2,128)(2,1)} %param.4) | copy-start | bytes 3076
  109.9 6.9 %copy-start = (bf16[1,1024,256]{2,1,0:T(8,128)(2,1)S(1)}, bf16[1,1024,256]{2,1,0:T(8,128)(2,1)}, u32[]{:S(2)}) copy-start(bf16[1,1024,256]{2,1,0:T(8,128)(2,1)} %param.6) | copy-start | bytes 1572868
  109.9 52.8 %all-to-all-start = ((bf16[16,64,1024]{2,1,0:T(8,128)(2,1)}), bf16[16,64,1024]{2,1,0:T(8,128)(2,1)S(1)}, u32[]{:S(2)}, u32[]{:S(2)}) async-start(bf16[16,64,1024]{2,1,0:T(8,128)(2,1)} %bitcast.62), calls=%async_computation | async-start | bytes 4194304 | tf_op jit(solution)/shard_map/all_to_all | solution.py:17
  167.6 11.7 %copy-start.1 = (bf16[1024,256]{1,0:T(8,128)(2,1)S(1)}, bf16[1024,256]{1,0:T(8,128)(2,1)}, u32[]{:S(2)}) copy-start(bf16[1024,256]{1,0:T(8,128)(2,1)} %param.7) | copy-start | bytes 1572868
  172.9 19.8 %all-to-all-start.1 = ((bf16[16,2,8192]{2,1,0:T(2,128)(2,1)}), bf16[16,2,8192]{2,1,0:T(2,128)(2,1)S(1)}, u32[]{:S(2)}, u32[]{:S(2)}) async-start(bf16[16,2,8192]{2,1,0:T(2,128)(2,1)} %reshape.121), calls=%async_computation.1 | async-start | bytes 1048576 | tf_op jit(solution)/shard_map/all_to_all | solution.py:40
  179.3 193.8 %all-reduce.2.cloned.1.call-start = ((), (), s32[]{:S(2)}) async-start(), calls=%async_computation.2 | async-start | bytes 131072 | tf_op jit(solution)/shard_map/psum | solution.py:54
Sparse Core Ops, SparseCore 0:
  284.4 88.6 all-reduce.1
where the time goes:
time: 382 us; the launch traced here: 381 us
  waiting for transfers between devices  147 us (38%)
  matrix products  109 us (29%)
  local copies, waits for them, and re-layouts  74.3 us (19%)
  blocking collectives  18.9 us (5%)
  between operations  14.2 us (4%)
  starting transfers between devices  13.3 us (3%)
  other arithmetic  4.9 us (1%)
    psum x1, waiting for transfers between devices, per_device(): summed = lax.psum(partial_value, 'wide')  87.8 us
    dot_general x1, matrix products, per_device(): jnp.dot(tile_green, chol_flat.T, preferred_element_type=jnp.float32)  80 us
    unnamed x14, local copies, waits for them, and re-layouts  64.8 us
    all_to_all x1, waiting for transfers between devices, per_device(): lax.all_to_all(generator, 'wide', split_axis=0, concat_axis=1, tiled=True)  45.6 us
    dot_general x1, matrix products, per_device(): jnp.dot(all_fields, chol_flat, preferred_element_type=jnp.float32)  22.8 us
    all_gather x1, blocking collectives, per_device(): all_fields = lax.all_gather(fields, 'wide', axis=0, tiled=True)  18.9 us
    all_to_all x1, waiting for transfers between devices, per_device(): lax.all_to_all(new_orbitals, 'wide', split_axis=1, concat_axis=0, tiled=T...  13.3 us
    another operation x1, local copies, waits for them, and re-layouts, per_device(): tile_green.reshape(all_walk, rows, 2, width).transpose(0, 2, 1, 3)  7.78 us
  transfers between devices with their start and end apart: 3, of which 3 were waited for; matrix products, arithmetic and copies ran while one was open for 0% of the time, Pallas kernels for 0%

commit v1 on v0

--- a/solution.py
+++ b/solution.py
@@ -51,7 +51,9 @@
     partial_value = jnp.dot(tile_green, chol_flat.T, preferred_element_type=jnp.float32).reshape(
         all_walk, 2, vectors
     )
-    summed = lax.psum(partial_value, "wide")
+    summed = partial_value
+    for hop in (1, 2, 4, 8):
+        summed = summed + lax.ppermute(summed, "wide", [(dev, dev ^ hop) for dev in range(16)])
     force_bias = lax.dynamic_slice_in_dim(
         summed, lax.axis_index("wide") * walk_local, walk_local, 0
     )

time: 382 us -> 295 us (0.77)
  waiting for transfers between devices: 147 us -> 70.5 us
  between operations: 14.2 us -> 0.81 us
    psum x1 -> x0, waiting for transfers between devices: 87.8 us -> none  [per_device(): summed = lax.psum(partial_value, 'wide')]
    ppermute x0 -> x4, waiting for transfers between devices: none -> 11.5 us  [per_device(): lax.ppermute(summed, 'wide', [(dev, dev ^ hop) for dev in range(16)])]
  transfers between devices with their start and end apart: 3 -> 6, of which waited for: 3 -> 6; matrix products, arithmetic and copies ran while one was open for 0% -> 0% of each run, Pallas kernels for 0% -> 0%
where the time goes in v1:
time: 295 us; the launch traced here: 294 us
  matrix products  108 us (37%)
  local copies, waits for them, and re-layouts  73.5 us (25%)
  waiting for transfers between devices  70.5 us (24%)
  blocking collectives  18.9 us (6%)
  starting transfers between devices  16.5 us (6%)
  other arithmetic  4.98 us (2%)
    dot_general x1, matrix products, per_device(): jnp.dot(tile_green, chol_flat.T, preferred_element_type=jnp.float32)  79.4 us
    unnamed x14, local copies, waits for them, and re-layouts  64.8 us
    all_to_all x1, waiting for transfers between devices, per_device(): lax.all_to_all(generator, 'wide', split_axis=0, concat_axis=1, tiled=True)  45.6 us
    dot_general x1, matrix products, per_device(): jnp.dot(all_fields, chol_flat, preferred_element_type=jnp.float32)  22.8 us
    all_gather x1, blocking collectives, per_device(): all_fields = lax.all_gather(fields, 'wide', axis=0, tiled=True)  18.9 us
    all_to_all x1, waiting for transfers between devices, per_device(): lax.all_to_all(new_orbitals, 'wide', split_axis=1, concat_axis=0, tiled=T...  13.4 us
    ppermute x4, waiting for transfers between devices, per_device(): lax.ppermute(summed, 'wide', [(dev, dev ^ hop) for dev in range(16)])  11.5 us
    another operation x1, local copies, waits for them, and re-layouts, per_device(): tile_green.reshape(all_walk, rows, 2, width).transpose(0, 2, 1, 3)  7.83 us
  transfers between devices with their start and end apart: 6, of which 6 were waited for; matrix products, arithmetic and copies ran while one was open for 0% of the time, Pallas kernels for 0%

profile of v1, /device:TPU:8, one launch (start us, length us, event | category | flops | bytes accessed | tf_op | source)
XLA Modules:
  0.0 293.5 jit_solution(1017835121993209400)
XLA Ops:
  0.6 58.5 %copy.31 = bf16[64,8,64,1024]{3,1,2,0:T(8,128)(2,1)} copy(bf16[64,8,64,1024]{3,2,1,0:T(8,128)(2,1)} %bitcast.19) | data formatting | bytes 134217728
  59.2 18.9 %all-gather = bf16[16,1,512]{2,1,0:T(2,128)(2,1)S(1)} all-gather(bf16[1,1,512]{2,1,0:T(2,128)(2,1)S(1)} %bitcast.65), channel_id=1, replica_groups=mesh['groups'=2,'wide'=16] {'wide'}, dimensions={0}, use_global_device_ids=true | all-gather | bytes 17408 | tf_op jit(solution)/shard_map/all_gather | solution.py:10
  78.1 22.8 %convolution_convert_fusion = bf16[16,65536]{1,0:T(8,128)(2,1)S(1)} fusion(bf16[512,65536]{1,0:T(8,128)(2,1)} %bitcast.20, bf16[16,1,512]{2,1,0:T(2,128)(2,1)S(1)} %all-gather), kind=kOutput, calls=%fused_computation | convolution fusion | flops 1074790400 | bytes 69222400 | tf_op jit(solution)/shard_map/dot_general | solution.py:13
  100.8 2.5 copy.32
  103.3 6.9 %all-to-all-start = ((bf16[16,64,1024]{2,1,0:T(8,128)(2,1)}), bf16[16,64,1024]{2,1,0:T(8,128)(2,1)S(1)}, u32[]{:S(2)}, u32[]{:S(2)}) async-start(bf16[16,64,1024]{2,1,0:T(8,128)(2,1)} %bitcast.62), calls=%async_computation | async-start | bytes 4194304 | tf_op jit(solution)/shard_map/all_to_all | solution.py:17
  110.2 0.2 copy.22
  110.5 45.6 %all-to-all-done = bf16[16,64,1024]{2,1,0:T(8,128)(2,1)S(1)} async-done(((bf16[16,64,1024]{2,1,0:T(8,128)(2,1)}), bf16[16,64,1024]{2,1,0:T(8,128)(2,1)S(1)}, u32[]{:S(2)}, u32[]{:S(2)}) %all-to-all-start) | async-done | bytes 2097184 | tf_op jit(solution)/shard_map/all_to_all | solution.py:17
  156.1 0.7 fusion.34
  157.0 0.7 fusion.28
  157.9 0.7 fusion.25
  158.8 0.7 fusion.23
  159.7 0.6 fusion.13
  160.2 0.9 copy.23
  161.1 0.5 broadcast.24
  161.6 3.8 %reduce = bf16[1024,256]{1,0:T(8,128)(2,1)S(1)} reduce(bf16[1024,1,256]{2,1,0:T(2,128)(2,1)S(1)} %bitcast.63, bf16[]{:T(256)} %broadcast.24), dimensions={1}, to_apply=%bitcast.50.reduce_sub_computation | reduce | bytes 1048578
  165.5 0.9 reshape.121
  166.4 6.4 %all-to-all-start.1 = ((bf16[16,2,8192]{2,1,0:T(2,128)(2,1)}), bf16[16,2,8192]{2,1,0:T(2,128)(2,1)S(1)}, u32[]{:S(2)}, u32[]{:S(2)}) async-start(bf16[16,2,8192]{2,1,0:T(2,128)(2,1)} %reshape.121), calls=%async_computation.1 | async-start | bytes 1048576 | tf_op jit(solution)/shard_map/all_to_all | solution.py:40
  172.9 13.4 %all-to-all-done.1 = bf16[16,2,8192]{2,1,0:T(2,128)(2,1)S(1)} async-done(((bf16[16,2,8192]{2,1,0:T(2,128)(2,1)}), bf16[16,2,8192]{2,1,0:T(2,128)(2,1)S(1)}, u32[]{:S(2)}, u32[]{:S(2)}) %all-to-all-start.1) | async-done | bytes 524320 | tf_op jit(solution)/shard_map/all_to_all | solution.py:40
  186.2 0.5 reshape.122
  186.8 3.2 %convolution_convert_fusion.1 = bf16[1024,2048]{1,0:T(8,128)(2,1)} fusion(bf16[128,1024]{0,1:T(8,128)(2,1)S(1)} %get-tuple-element.24, bf16[128,1024]{0,1:T(8,128)(2,1)S(1)} %get-tuple-element.23, bf16[128,1024]{0,1:T(8,128)(2,1)S(1)} %fusion.48, bf16[1,1024,256]{2,0,1:T(2,128)(2,1)S(1)} %bitcast.64), kind=kOutput, calls=%fused_computation.6 | convolution fusion | flops 1080033280 | bytes 5505024 | tf_op jit(solution)/shard_map/dot_general | solution.py:43
  190.0 7.8 %reshape_reshape.3 = bf16[16,64,2,1024]{3,2,1,0:T(2,128)(2,1)} reshape(bf16[1024,2048]{1,0:T(8,128)(2,1)} %convolution_convert_fusion.1) | data formatting | bytes 8388608 | tf_op jit(solution)/shard_map/reshape;reshape | solution.py:47
  197.8 79.4 %fusion.5 = f32[16,2,512]{2,0,1:T(8,128)S(1)} fusion(bf16[512,64,1024]{2,1,0:T(8,128)(2,1)} %param.5, bf16[16,64,2,1024]{3,2,1,0:T(2,128)(2,1)} %reshape_reshape.3), kind=kOutput, calls=%fused_computation.7 | convolution fusion | flops 2147483648 | bytes 71368704 | tf_op jit(solution)/shard_map/dot_general | solution.py:51
  277.2 0.8 collective-permute-start
  278.0 0.9 collective-permute-done
  278.9 1.0 collective-permute-start.1
  279.9 3.4 %collective-permute-done.1 = f32[16,2,512]{2,0,1:T(8,128)S(1)} collective-permute-done((f32[16,2,512]{2,0,1:T(8,128)S(1)}, f32[16,2,512]{2,0,1:T(8,128)S(1)}, u32[]{:S(2)}, u32[]{:S(2)}) %collective-permute-start.1) | collective-permute-done | bytes 65568 | tf_op jit(solution)/shard_map/ppermute | solution.py:56
  283.4 0.5 collective-permute-start.2
  283.8 3.9 %collective-permute-done.2 = f32[16,2,512]{2,0,1:T(8,128)S(1)} collective-permute-done((f32[16,2,512]{2,0,1:T(8,128)S(1)}, f32[16,2,512]{2,0,1:T(8,128)S(1)}, u32[]{:S(2)}, u32[]{:S(2)}) %collective-permute-start.2) | collective-permute-done | bytes 65568 | tf_op jit(solution)/shard_map/ppermute | solution.py:56
  287.7 0.9 collective-permute-start.3
  288.6 1.0 copy.26
  289.6 3.3 %collective-permute-done.3 = f32[16,2,512]{2,0,1:T(8,128)S(1)} collective-permute-done((f32[16,2,512]{2,0,1:T(8,128)S(1)}, f32[16,2,512]{2,0,1:T(8,128)S(1)}, u32[]{:S(2)}, u32[]{:S(2)}) %collective-permute-start.3) | collective-permute-done | bytes 65568 | tf_op jit(solution)/shard_map/ppermute | solution.py:56
  292.9 0.6 copy.27
  (17 shorter events, 0.7 us)
Async XLA Ops:
  0.6 58.6 %copy-start.2 = (bf16[1,512]{1,0:T(2,128)(2,1)S(1)}, bf16[1,512]{1,0:T(2,128)(2,1)}, u32[]{:S(2)}) copy-start(bf16[1,512]{1,0:T(2,128)(2,1)} %param.4) | copy-start | bytes 3076
  103.3 6.9 %copy-start = (bf16[1,1024,256]{2,1,0:T(8,128)(2,1)S(1)}, bf16[1,1024,256]{2,1,0:T(8,128)(2,1)}, u32[]{:S(2)}) copy-start(bf16[1,1024,256]{2,1,0:T(8,128)(2,1)} %param.6) | copy-start | bytes 1572868
  103.3 52.8 %all-to-all-start = ((bf16[16,64,1024]{2,1,0:T(8,128)(2,1)}), bf16[16,64,1024]{2,1,0:T(8,128)(2,1)S(1)}, u32[]{:S(2)}, u32[]{:S(2)}) async-start(bf16[16,64,1024]{2,1,0:T(8,128)(2,1)} %bitcast.62), calls=%async_computation | async-start | bytes 4194304 | tf_op jit(solution)/shard_map/all_to_all | solution.py:17
  161.1 11.6 %copy-start.1 = (bf16[1024,256]{1,0:T(8,128)(2,1)S(1)}, bf16[1024,256]{1,0:T(8,128)(2,1)}, u32[]{:S(2)}) copy-start(bf16[1024,256]{1,0:T(8,128)(2,1)} %param.7) | copy-start | bytes 1572868
  166.4 19.9 %all-to-all-start.1 = ((bf16[16,2,8192]{2,1,0:T(2,128)(2,1)}), bf16[16,2,8192]{2,1,0:T(2,128)(2,1)S(1)}, u32[]{:S(2)}, u32[]{:S(2)}) async-start(bf16[16,2,8192]{2,1,0:T(2,128)(2,1)} %reshape.121), calls=%async_computation.1 | async-start | bytes 1048576 | tf_op jit(solution)/shard_map/all_to_all | solution.py:40
  277.2 1.7 collective-permute-start
  278.9 4.4 %collective-permute-start.1 = (f32[16,2,512]{2,0,1:T(8,128)S(1)}, f32[16,2,512]{2,0,1:T(8,128)S(1)}, u32[]{:S(2)}, u32[]{:S(2)}) collective-permute-start(f32[16,2,512]{2,0,1:T(8,128)S(1)} %add.35), channel_id=1, source_target_pairs={{0,2},{1,3},{2,0},{3,1},{4,6},{5,7},{6,4},{7,5},{8,10},{9,11},{10,... | collective-permute-start | bytes 196616 | tf_op jit(solution)/shard_map/ppermute | solution.py:56
  283.4 4.3 %collective-permute-start.2 = (f32[16,2,512]{2,0,1:T(8,128)S(1)}, f32[16,2,512]{2,0,1:T(8,128)S(1)}, u32[]{:S(2)}, u32[]{:S(2)}) collective-permute-start(f32[16,2,512]{2,0,1:T(8,128)S(1)} %add.36), channel_id=1, source_target_pairs={{0,4},{1,5},{2,6},{3,7},{4,0},{5,1},{6,2},{7,3},{8,12},{9,13},{10,... | collective-permute-start | bytes 196616 | tf_op jit(solution)/shard_map/ppermute | solution.py:56
  287.7 5.2 %collective-permute-start.3 = (f32[16,2,512]{2,0,1:T(8,128)S(1)}, f32[16,2,512]{2,0,1:T(8,128)S(1)}, u32[]{:S(2)}, u32[]{:S(2)}) collective-permute-start(f32[16,2,512]{2,0,1:T(8,128)S(1)} %add.37), channel_id=1, source_target_pairs={{0,8},{1,9},{2,10},{3,11},{4,12},{5,13},{6,14},{7,15},{8,0},{9,1},... | collective-permute-start | bytes 196616 | tf_op jit(solution)/shard_map/ppermute | solution.py:56
